TPU v7x, 256 devices: a whole 4x4x8 slice. The times are simulated.
256 devices in a mesh: section: 8 (over y, core), chan: 32 (over z, x).
Axes of the slice: x: 4, y: 4, z: 8, core: 2. Of those that a mesh axis runs over, the one named last changes fastest.
Arguments:
- prompt: bfloat16 [192, 8192], P(None, 'chan'), may hold values from -6 to 6
- norm_gain: bfloat16 [8, 8192], P('section', 'chan'), may hold values from 0.5 to 1.5
- in_weight: bfloat16 [8, 8192, 3, 8192], P('section', None, None, 'chan'), may hold values from -0.0625 to 0.0625
- feat_taps: float32 [8, 3, 3, 8192], P('section', None, None, 'chan'), may hold values from -3 to 3
- fir_taps: float32 [8, 128, 512], P('section', None, 'chan'), may hold values from -0.5 to 0.5
- residues: float32 [8, 16, 512], P('section', None, 'chan'), may hold values from -0.2 to 0.2
- decay: float32 [8, 16, 512], P('section', None, 'chan'), may hold values from 0.002 to 0.1
Outputs:
- section_out: bfloat16 [8, 192, 8192], P('section', None, 'chan')
All inputs are finite; a program needn't handle non-finite values.
Results may differ from a plain program's by a relative error of at most 0.019.
Values may be sent and summed in bfloat16 or wider, within the bound.
A program may use at most 128 MiB of HBM per device.

v0:
```python
import jax
import jax.numpy as jnp
from jax import lax
from jax.sharding import PartitionSpec as P

BLOCK_TOK = 64
NBLOCKS = 3
EPSILON = 1e-06


def shifted(value, axis, steps):
    count = lax.axis_size(axis)
    initial, last = (max(0, -steps), min(count, count - steps))
    return lax.ppermute(value, axis, [(source, source + steps) for source in range(initial, last)])


def body(prompt, norm_gain, in_weight, feat_taps, fir_taps, residues, decay):
    block_len = BLOCK_TOK
    num_blocks = NBLOCKS
    width = in_weight.shape[1]
    local = prompt.shape[1]
    groups_local = fir_taps.shape[2]
    group_size = local // groups_local
    fir_len = fir_taps.shape[1]
    sections = lax.axis_size("section")
    section_idx = lax.axis_index("section")
    is_medium = section_idx % 2 == 0
    weight = in_weight[0].reshape(width, 3 * local)
    tap_rows = feat_taps[0]
    fir_section = fir_taps[0]
    residue_section = residues[0]
    rate_section = decay[0]
    out_pos = jnp.arange(block_len)
    in_pos = jnp.arange(fir_len + block_len)
    fir_lag = out_pos[:, None] + fir_len - in_pos[None, :]
    fir_ok = (fir_lag >= 0) & (fir_lag < fir_len)
    fir_table = jnp.where(fir_ok[None], fir_section.T[:, jnp.clip(fir_lag, 0, fir_len - 1)], 0.0)
    inner_lag = out_pos[:, None] - (in_pos[None, :] - fir_len)
    inner_ok = (inner_lag >= 0) & (in_pos[None, :] >= fir_len)
    lag_values = out_pos.astype(jnp.float32)
    powers = jnp.exp(-rate_section[None, :, :] * lag_values[:, None, None])
    modal = jnp.einsum("ng,jng->jg", residue_section, powers, precision=lax.Precision.HIGHEST)
    modal_table = jnp.where(inner_ok[None], modal.T[:, jnp.clip(inner_lag, 0, block_len - 1)], 0.0)
    toeplitz = jnp.where(is_medium, fir_table, modal_table)
    carry_coef = residue_section[None] * jnp.exp(
        -rate_section[None] * (lag_values + 1.0)[:, None, None]
    )
    carry_coef = jnp.where(is_medium, 0.0, carry_coef)
    feed_coef = jnp.exp(-rate_section[None] * (block_len - 1.0 - lag_values)[:, None, None])
    block_decay = jnp.exp(-rate_section * block_len)

    def add_rows(shard_piece):
        return jnp.dot(shard_piece, weight, preferred_element_type=jnp.float32)

    def turn(carried, turn_index):
        incoming, proj_cache, kv_cache, modal_state, out_buffer = carried
        which = turn_index - section_idx
        is_live = (which >= 0) & (which < num_blocks)
        begin_row = jnp.clip(which, 0, num_blocks - 1) * block_len
        first_rows = lax.dynamic_slice_in_dim(prompt, begin_row, block_len, 0)
        rows_in = jnp.where(section_idx == 0, first_rows, incoming)
        inputs_f = rows_in.astype(jnp.float32)
        partial_sq = jnp.sum(inputs_f * inputs_f, axis=1)
        squares = lax.psum(partial_sq, "chan")
        normed = (
            inputs_f * lax.rsqrt(squares[:, None] / width + EPSILON) * norm_gain.astype(jnp.float32)
        ).astype(jnp.bfloat16)
        projected = add_rows(lax.all_gather(normed, "chan", axis=1, tiled=True))
        projected = projected.reshape(block_len, 3, local)
        extended = jnp.concatenate([proj_cache, projected], axis=0)
        features = (
            tap_rows[0] * extended[2:] + tap_rows[1] * extended[1:-1] + tap_rows[2] * extended[:-2]
        )
        product_kv = features[:, 1] * features[:, 2]
        window = jnp.concatenate([kv_cache, product_kv], axis=0)
        grouped = window.reshape(fir_len + block_len, groups_local, group_size)
        convolved = jnp.einsum("gts,sgk->tgk", toeplitz, grouped, precision=lax.Precision.HIGHEST)
        convolved = convolved + jnp.einsum(
            "tng,ngk->tgk", carry_coef, modal_state, precision=lax.Precision.HIGHEST
        )
        new_state = block_decay[:, :, None] * modal_state + jnp.einsum(
            "tng,tgk->ngk", feed_coef, grouped[fir_len:], precision=lax.Precision.HIGHEST
        )
        result = (inputs_f + features[:, 0] * convolved.reshape(block_len, local)).astype(
            jnp.bfloat16
        )
        proj_cache = jnp.where(is_live, extended[block_len:], proj_cache)
        kv_cache = jnp.where(is_live, window[block_len:], kv_cache)
        modal_state = jnp.where(is_live, new_state, modal_state)
        out_buffer = jnp.where(
            is_live, lax.dynamic_update_slice_in_dim(out_buffer, result, begin_row, 0), out_buffer
        )
        passed = shifted(result, "section", 1)
        return ((passed, proj_cache, kv_cache, modal_state, out_buffer), None)

    initial = (
        jnp.zeros((block_len, local), jnp.bfloat16),
        jnp.zeros((2, 3, local), jnp.float32),
        jnp.zeros((fir_len, local), jnp.float32),
        jnp.zeros((residues.shape[1], groups_local, group_size), jnp.float32),
        jnp.zeros((block_len * num_blocks, local), jnp.bfloat16),
    )
    finals, unused = lax.scan(turn, initial, jnp.arange(num_blocks + sections - 1, dtype=jnp.int32))
    return finals[4][None]


def solution(mesh):
    return jax.shard_map(
        body,
        mesh=mesh,
        in_specs=(
            P(None, "chan"),
            P("section", "chan"),
            P("section", None, None, "chan"),
            P("section", None, None, "chan"),
            P("section", None, "chan"),
            P("section", None, "chan"),
            P("section", None, "chan"),
        ),
        out_specs=P("section", None, "chan"),
        check_vma=False,
    )
```

profile of v0, /device:TPU:1, one launch (start us, length us, event | category | flops | bytes accessed | tf_op | source)
XLA Modules:
  0.0 1730.6 jit_solution(16256413265977966794)
XLA Ops:
  7.2 16.7 copy.26
  23.9 16.7 copy.33
  41.1 41.1 %gather_fusion.1 = f32[12288,16]{1,0:T(8,128)} fusion(f32[16,64]{0,1:T(8,128)S(1)} %multiply_reduce_fusion, s32[12288]{0:T(1024)S(1)} %broadcast_clamp_fusion), kind=kCustom, calls=%fused_computation.1 | custom fusion | bytes 1622016 | tf_op jit(solution)/shard_map/gather | solution.py:43
  87.5 41.1 %gather_fusion = f32[12288,16]{1,0:T(8,128)} fusion(f32[16,128]{0,1:T(8,128)S(1)} %bitcast.82, s32[12288]{0:T(1024)S(1)} %broadcast_clamp_fusion.1), kind=kCustom, calls=%fused_computation | custom fusion | bytes 1622016 | tf_op jit(solution)/shard_map/gather | solution.py:37
  133.9 1589.2 %while.22 = (s32[]{:T(128)}, bf16[64,256]{1,0:T(8,128)(2,1)S(1)}, f32[2,3,256]{2,1,0:T(4,128)S(1)}, f32[128,256]{0,1:T(8,128)S(1)}, f32[16,16,16]{0,2,1:T(8,128)...) while((s32[]{:T(128)}, bf16[64,256]{1,0:T(8,128)(2,1)S(1)}, ...), condition=%wide.region_3.4_spmd.clone.clone.clone, body=%wide.region_0.3_spmd.clone.clone.clone.sunk | while | flops 850173312 | bytes 21374916 | solution.py:103
  136.1 64.3 %psum.12 = f32[64]{0:T(128)S(1)} all-reduce(f32[64]{0:T(128)S(1)} %get-tuple-element.554), channel_id=1, replica_groups=mesh['section'=8,'chan'=32] {'chan'}, use_global_device_ids=true, to_apply=%region_2.2 | all-reduce | flops 64 | bytes 512 | tf_op jit(solution)/shard_map/while/body/eval_jaxpr/psum | solution.py:64
  201.2 76.1 %all-gather.2.cloned.1.call-done = bf16[64,8192]{1,0:T(8,128)(2,1)} async-done(((bf16[64,256]{1,0:T(8,128)(2,1)}), bf16[64,8192]{1,0:T(8,128)(2,1)}) %all-gather.2.cloned.1.call-update) | async-done | bytes 1048592 | tf_op jit(solution)/shard_map/while/body/eval_jaxpr/all_gather | solution.py:68
  286.4 7.7 collective-permute-start
  297.3 59.9 %psum.12 = f32[64]{0:T(128)S(1)} all-reduce(f32[64]{0:T(128)S(1)} %get-tuple-element.554), channel_id=1, replica_groups=mesh['section'=8,'chan'=32] {'chan'}, use_global_device_ids=true, to_apply=%region_2.2 | all-reduce | flops 64 | bytes 512 | tf_op jit(solution)/shard_map/while/body/eval_jaxpr/psum | solution.py:64
  357.9 78.0 %all-gather.2.cloned.1.call-done = bf16[64,8192]{1,0:T(8,128)(2,1)} async-done(((bf16[64,256]{1,0:T(8,128)(2,1)}), bf16[64,8192]{1,0:T(8,128)(2,1)}) %all-gather.2.cloned.1.call-update) | async-done | bytes 1048592 | tf_op jit(solution)/shard_map/while/body/eval_jaxpr/all_gather | solution.py:68
  445.0 7.7 collective-permute-start
  455.9 59.9 %psum.12 = f32[64]{0:T(128)S(1)} all-reduce(f32[64]{0:T(128)S(1)} %get-tuple-element.554), channel_id=1, replica_groups=mesh['section'=8,'chan'=32] {'chan'}, use_global_device_ids=true, to_apply=%region_2.2 | all-reduce | flops 64 | bytes 512 | tf_op jit(solution)/shard_map/while/body/eval_jaxpr/psum | solution.py:64
  516.6 78.0 %all-gather.2.cloned.1.call-done = bf16[64,8192]{1,0:T(8,128)(2,1)} async-done(((bf16[64,256]{1,0:T(8,128)(2,1)}), bf16[64,8192]{1,0:T(8,128)(2,1)}) %all-gather.2.cloned.1.call-update) | async-done | bytes 1048592 | tf_op jit(solution)/shard_map/while/body/eval_jaxpr/all_gather | solution.py:68
  603.7 7.7 collective-permute-start
  614.6 59.9 %psum.12 = f32[64]{0:T(128)S(1)} all-reduce(f32[64]{0:T(128)S(1)} %get-tuple-element.554), channel_id=1, replica_groups=mesh['section'=8,'chan'=32] {'chan'}, use_global_device_ids=true, to_apply=%region_2.2 | all-reduce | flops 64 | bytes 512 | tf_op jit(solution)/shard_map/while/body/eval_jaxpr/psum | solution.py:64
  675.2 78.0 %all-gather.2.cloned.1.call-done = bf16[64,8192]{1,0:T(8,128)(2,1)} async-done(((bf16[64,256]{1,0:T(8,128)(2,1)}), bf16[64,8192]{1,0:T(8,128)(2,1)}) %all-gather.2.cloned.1.call-update) | async-done | bytes 1048592 | tf_op jit(solution)/shard_map/while/body/eval_jaxpr/all_gather | solution.py:68
  762.4 7.7 collective-permute-start
  773.3 59.9 %psum.12 = f32[64]{0:T(128)S(1)} all-reduce(f32[64]{0:T(128)S(1)} %get-tuple-element.554), channel_id=1, replica_groups=mesh['section'=8,'chan'=32] {'chan'}, use_global_device_ids=true, to_apply=%region_2.2 | all-reduce | flops 64 | bytes 512 | tf_op jit(solution)/shard_map/while/body/eval_jaxpr/psum | solution.py:64
  833.9 78.0 %all-gather.2.cloned.1.call-done = bf16[64,8192]{1,0:T(8,128)(2,1)} async-done(((bf16[64,256]{1,0:T(8,128)(2,1)}), bf16[64,8192]{1,0:T(8,128)(2,1)}) %all-gather.2.cloned.1.call-update) | async-done | bytes 1048592 | tf_op jit(solution)/shard_map/while/body/eval_jaxpr/all_gather | solution.py:68
  931.9 59.9 %psum.12 = f32[64]{0:T(128)S(1)} all-reduce(f32[64]{0:T(128)S(1)} %get-tuple-element.554), channel_id=1, replica_groups=mesh['section'=8,'chan'=32] {'chan'}, use_global_device_ids=true, to_apply=%region_2.2 | all-reduce | flops 64 | bytes 512 | tf_op jit(solution)/shard_map/while/body/eval_jaxpr/psum | solution.py:64
  992.6 78.0 %all-gather.2.cloned.1.call-done = bf16[64,8192]{1,0:T(8,128)(2,1)} async-done(((bf16[64,256]{1,0:T(8,128)(2,1)}), bf16[64,8192]{1,0:T(8,128)(2,1)}) %all-gather.2.cloned.1.call-update) | async-done | bytes 1048592 | tf_op jit(solution)/shard_map/while/body/eval_jaxpr/all_gather | solution.py:68
  1079.7 7.7 collective-permute-start
  1090.6 59.9 %psum.12 = f32[64]{0:T(128)S(1)} all-reduce(f32[64]{0:T(128)S(1)} %get-tuple-element.554), channel_id=1, replica_groups=mesh['section'=8,'chan'=32] {'chan'}, use_global_device_ids=true, to_apply=%region_2.2 | all-reduce | flops 64 | bytes 512 | tf_op jit(solution)/shard_map/while/body/eval_jaxpr/psum | solution.py:64
  1151.2 78.0 %all-gather.2.cloned.1.call-done = bf16[64,8192]{1,0:T(8,128)(2,1)} async-done(((bf16[64,256]{1,0:T(8,128)(2,1)}), bf16[64,8192]{1,0:T(8,128)(2,1)}) %all-gather.2.cloned.1.call-update) | async-done | bytes 1048592 | tf_op jit(solution)/shard_map/while/body/eval_jaxpr/all_gather | solution.py:68
  1249.3 59.9 %psum.12 = f32[64]{0:T(128)S(1)} all-reduce(f32[64]{0:T(128)S(1)} %get-tuple-element.554), channel_id=1, replica_groups=mesh['section'=8,'chan'=32] {'chan'}, use_global_device_ids=true, to_apply=%region_2.2 | all-reduce | flops 64 | bytes 512 | tf_op jit(solution)/shard_map/while/body/eval_jaxpr/psum | solution.py:64
  1309.9 78.0 %all-gather.2.cloned.1.call-done = bf16[64,8192]{1,0:T(8,128)(2,1)} async-done(((bf16[64,256]{1,0:T(8,128)(2,1)}), bf16[64,8192]{1,0:T(8,128)(2,1)}) %all-gather.2.cloned.1.call-update) | async-done | bytes 1048592 | tf_op jit(solution)/shard_map/while/body/eval_jaxpr/all_gather | solution.py:68
  1397.0 7.7 collective-permute-start
  1407.9 59.9 %psum.12 = f32[64]{0:T(128)S(1)} all-reduce(f32[64]{0:T(128)S(1)} %get-tuple-element.554), channel_id=1, replica_groups=mesh['section'=8,'chan'=32] {'chan'}, use_global_device_ids=true, to_apply=%region_2.2 | all-reduce | flops 64 | bytes 512 | tf_op jit(solution)/shard_map/while/body/eval_jaxpr/psum | solution.py:64
  1468.6 78.0 %all-gather.2.cloned.1.call-done = bf16[64,8192]{1,0:T(8,128)(2,1)} async-done(((bf16[64,256]{1,0:T(8,128)(2,1)}), bf16[64,8192]{1,0:T(8,128)(2,1)}) %all-gather.2.cloned.1.call-update) | async-done | bytes 1048592 | tf_op jit(solution)/shard_map/while/body/eval_jaxpr/all_gather | solution.py:68
  1566.6 59.9 %psum.12 = f32[64]{0:T(128)S(1)} all-reduce(f32[64]{0:T(128)S(1)} %get-tuple-element.554), channel_id=1, replica_groups=mesh['section'=8,'chan'=32] {'chan'}, use_global_device_ids=true, to_apply=%region_2.2 | all-reduce | flops 64 | bytes 512 | tf_op jit(solution)/shard_map/while/body/eval_jaxpr/psum | solution.py:64
  1627.2 78.0 %all-gather.2.cloned.1.call-done = bf16[64,8192]{1,0:T(8,128)(2,1)} async-done(((bf16[64,256]{1,0:T(8,128)(2,1)}), bf16[64,8192]{1,0:T(8,128)(2,1)}) %all-gather.2.cloned.1.call-update) | async-done | bytes 1048592 | tf_op jit(solution)/shard_map/while/body/eval_jaxpr/all_gather | solution.py:68
  1714.4 7.7 collective-permute-start
  (291 shorter events, 158.0 us)
Async XLA Ops:
  23.9 16.7 copy-start.4
  23.9 16.8 copy-start.1
  40.6 46.6 %copy-start.3 = (f32[1,128,16]{1,2,0:T(8,128)S(1)}, f32[1,128,16]{1,2,0:T(8,128)}, u32[]{:S(2)}) copy-start(f32[1,128,16]{1,2,0:T(8,128)} %param.13) | copy-start | bytes 24580
  82.3 51.6 %copy-start.2 = (bf16[1,256]{1,0:T(2,128)(2,1)S(1)}, bf16[1,256]{1,0:T(2,128)(2,1)}, u32[]{:S(2)}) copy-start(bf16[1,256]{1,0:T(2,128)(2,1)} %param.10) | copy-start | bytes 1540
  133.9 143.3 %all-gather.2.cloned.1.call-start = ((), (), s32[]{:S(2)}) async-start(), calls=%async_computation | async-start | bytes 1081344 | tf_op jit(solution)/shard_map/while/body/eval_jaxpr/all_gather | solution.py:68
  286.4 8.7 collective-permute-start
  295.1 140.8 %all-gather.2.cloned.1.call-start = ((), (), s32[]{:S(2)}) async-start(), calls=%async_computation | async-start | bytes 1081344 | tf_op jit(solution)/shard_map/while/body/eval_jaxpr/all_gather | solution.py:68
  445.0 8.7 collective-permute-start
  453.8 140.8 %all-gather.2.cloned.1.call-start = ((), (), s32[]{:S(2)}) async-start(), calls=%async_computation | async-start | bytes 1081344 | tf_op jit(solution)/shard_map/while/body/eval_jaxpr/all_gather | solution.py:68
  603.7 8.7 collective-permute-start
  612.5 140.8 %all-gather.2.cloned.1.call-start = ((), (), s32[]{:S(2)}) async-start(), calls=%async_computation | async-start | bytes 1081344 | tf_op jit(solution)/shard_map/while/body/eval_jaxpr/all_gather | solution.py:68
  762.4 8.7 collective-permute-start
  771.1 140.8 %all-gather.2.cloned.1.call-start = ((), (), s32[]{:S(2)}) async-start(), calls=%async_computation | async-start | bytes 1081344 | tf_op jit(solution)/shard_map/while/body/eval_jaxpr/all_gather | solution.py:68
  921.0 8.7 collective-permute-start
  929.8 140.8 %all-gather.2.cloned.1.call-start = ((), (), s32[]{:S(2)}) async-start(), calls=%async_computation | async-start | bytes 1081344 | tf_op jit(solution)/shard_map/while/body/eval_jaxpr/all_gather | solution.py:68
  1079.7 8.7 collective-permute-start
  1088.5 140.8 %all-gather.2.cloned.1.call-start = ((), (), s32[]{:S(2)}) async-start(), calls=%async_computation | async-start | bytes 1081344 | tf_op jit(solution)/shard_map/while/body/eval_jaxpr/all_gather | solution.py:68
  1238.4 8.7 collective-permute-start
  1247.1 140.8 %all-gather.2.cloned.1.call-start = ((), (), s32[]{:S(2)}) async-start(), calls=%async_computation | async-start | bytes 1081344 | tf_op jit(solution)/shard_map/while/body/eval_jaxpr/all_gather | solution.py:68
  1397.0 8.7 collective-permute-start
  1405.8 140.8 %all-gather.2.cloned.1.call-start = ((), (), s32[]{:S(2)}) async-start(), calls=%async_computation | async-start | bytes 1081344 | tf_op jit(solution)/shard_map/while/body/eval_jaxpr/all_gather | solution.py:68
  1555.7 8.7 collective-permute-start
  1564.4 140.8 %all-gather.2.cloned.1.call-start = ((), (), s32[]{:S(2)}) async-start(), calls=%async_computation | async-start | bytes 1081344 | tf_op jit(solution)/shard_map/while/body/eval_jaxpr/all_gather | solution.py:68
  1714.4 8.7 collective-permute-start
  1723.1 0.6 copy-start
Sparse Core Ops, SparseCore 0:
  201.3 75.9 all-gather.1
  358.0 77.8 all-gather.1
  516.6 77.8 all-gather.1
  675.3 77.8 all-gather.1
  834.0 77.8 all-gather.1
  992.6 77.8 all-gather.1
  1151.3 77.8 all-gather.1
  1310.0 77.8 all-gather.1
  1468.6 77.8 all-gather.1
  1627.3 77.8 all-gather.1
where the time goes:
time: 1730 us
  waiting for transfers between devices  783 us (45%)
  blocking collectives  603 us (35%)
  local copies, waits for them, and re-layouts  136 us (8%)
  matrix products  88.7 us (5%)
  starting transfers between devices  77.4 us (4%)
  other arithmetic  20.9 us (1%)
    all_gather x10, waiting for transfers between devices, turn(): projected = add_rows(lax.all_gather(normed, 'chan', axis=1, tiled=True))  778 us
    psum x10, blocking collectives, turn(): squares = lax.psum(partial_sq, 'chan')  603 us
    ppermute x10, starting transfers between devices, shifted(): lax.ppermute(value, axis, [(source, source + steps) for source in range(i...  77.3 us
    dot_general x10, matrix products, add_rows(): return jnp.dot(shard_piece, weight, preferred_element_type=jnp.float32)  71.6 us
    gather x2, local copies, waits for them, and re-layouts, body(): modal.T[:, jnp.clip(inner_lag, 0, block_len - 1)]  46 us
    gather x2, local copies, waits for them, and re-layouts, body(): fir_section.T[:, jnp.clip(fir_lag, 0, fir_len - 1)]  46 us
    unnamed x16, local copies, waits for them, and re-layouts  34.9 us
  transfers between devices with their start and end apart: 20, of which 20 were waited for; matrix products, arithmetic and copies ran while one was open for 0% of the time, Pallas kernels for 0%

commit v1 on v0

--- a/solution.py
+++ b/solution.py
@@ -6,6 +6,11 @@
 BLOCK_TOK = 64
 NBLOCKS = 3
 EPSILON = 1e-06
+
+
+def exchange_gather(block, name, along):
+    sent = jnp.stack([block] * lax.axis_size(name))
+    return jnp.concatenate(lax.all_to_all(sent, name, 0, 0), axis=along)
 
 
 def shifted(value, axis, steps):
@@ -65,7 +70,7 @@
         normed = (
             inputs_f * lax.rsqrt(squares[:, None] / width + EPSILON) * norm_gain.astype(jnp.float32)
         ).astype(jnp.bfloat16)
-        projected = add_rows(lax.all_gather(normed, "chan", axis=1, tiled=True))
+        projected = add_rows(exchange_gather(normed, "chan", 1))
         projected = projected.reshape(block_len, 3, local)
         extended = jnp.concatenate([proj_cache, projected], axis=0)
         features = (

time: 1730 us -> 1270 us (0.73)
  waiting for transfers between devices: 783 us -> 199 us
  starting transfers between devices: 77.4 us -> 230 us
  blocking collectives: 603 us -> 579 us
    all_gather x10 -> x0, waiting for transfers between devices: 778 us -> none  [turn(): projected = add_rows(lax.all_gather(normed, 'chan', axis=1, tiled=True))]
    all_to_all x0 -> x10, waiting for transfers between devices: none -> 195 us  [exchange_gather(): return jnp.concatenate(lax.all_to_all(sent, name, 0, 0), axis=along)]
    ppermute x10, starting transfers between devices: 77.3 us -> 177 us  [shifted(): lax.ppermute(value, axis, [(source, source + steps) for source in range(i...]
    all_to_all x0 -> x10, starting transfers between devices: none -> 53 us  [exchange_gather(): return jnp.concatenate(lax.all_to_all(sent, name, 0, 0), axis=along)]
    psum x10, blocking collectives: 603 us -> 579 us  [turn(): squares = lax.psum(partial_sq, 'chan')]
where the time goes in v1:
time: 1270 us; the launch traced here: 1260 us
  blocking collectives  579 us (46%)
  starting transfers between devices  230 us (18%)
  waiting for transfers between devices  199 us (16%)
  local copies, waits for them, and re-layouts  148 us (12%)
  matrix products  85.5 us (7%)
  other arithmetic  14.7 us (1%)
    psum x10, blocking collectives, turn(): squares = lax.psum(partial_sq, 'chan')  579 us
    all_to_all x10, waiting for transfers between devices, exchange_gather(): return jnp.concatenate(lax.all_to_all(sent, name, 0, 0), axis=along)  195 us
    ppermute x10, starting transfers between devices, shifted(): lax.ppermute(value, axis, [(source, source + steps) for source in range(i...  177 us
    dot_general x10, matrix products, add_rows(): return jnp.dot(shard_piece, weight, preferred_element_type=jnp.float32)  68.4 us
    all_to_all x10, starting transfers between devices, exchange_gather(): return jnp.concatenate(lax.all_to_all(sent, name, 0, 0), axis=along)  53 us
    gather x2, local copies, waits for them, and re-layouts, body(): modal.T[:, jnp.clip(inner_lag, 0, block_len - 1)]  46.2 us
    gather x2, local copies, waits for them, and re-layouts, body(): fir_section.T[:, jnp.clip(fir_lag, 0, fir_len - 1)]  46.2 us
    unnamed x16, local copies, waits for them, and re-layouts  35 us
  transfers between devices with their start and end apart: 20, of which 20 were waited for; matrix products, arithmetic and copies ran while one was open for 0% of the time, Pallas kernels for 0%

profile of v1, /device:TPU:1, one launch (start us, length us, event | category | flops | bytes accessed | tf_op | source)
XLA Modules:
  0.0 1264.2 jit_solution(18432028588006488724)
XLA Ops:
  0.7 16.7 %copy.38 = bf16[1,8192,3,256]{1,3,2,0:T(8,128)(2,1)} copy(bf16[1,8192,3,256]{3,1,2,0:T(8,128)(2,1)} %param.11) | data formatting | bytes 25165824 | tf_op args[2]
  34.6 41.3 %gather_fusion.1 = f32[12288,16]{1,0:T(8,128)} fusion(f32[16,64]{0,1:T(8,128)S(1)} %multiply_reduce_fusion, s32[12288]{0:T(1024)S(1)} %broadcast_clamp_fusion), kind=kCustom, calls=%fused_computation.1 | custom fusion | bytes 1622016 | tf_op jit(solution)/shard_map/gather | solution.py:48
  81.2 41.3 %gather_fusion = f32[12288,16]{1,0:T(8,128)} fusion(f32[16,128]{0,1:T(8,128)S(1)} %bitcast.89, s32[12288]{0:T(1024)S(1)} %broadcast_clamp_fusion.1), kind=kCustom, calls=%fused_computation | custom fusion | bytes 1622016 | tf_op jit(solution)/shard_map/gather | solution.py:42
  127.8 1135.8 %while.22 = (s32[]{:T(128)}, bf16[64,256]{1,0:T(8,128)(2,1)S(1)}, f32[2,3,256]{2,1,0:T(4,128)S(1)}, f32[128,256]{0,1:T(8,128)S(1)}, f32[16,16,16]{0,2,1:T(8,128)...) while((s32[]{:T(128)}, bf16[64,256]{1,0:T(8,128)(2,1)S(1)}, ...), condition=%wide.region_3.4_spmd.clone.clone.clone, body=%wide.region_0.3_spmd.clone.clone.clone.sunk | while | flops 850173312 | bytes 24455100 | solution.py:108
  129.8 64.3 %psum.12 = f32[64]{0:T(128)S(1)} all-reduce(f32[64]{0:T(128)S(1)} %get-tuple-element.574), channel_id=1, replica_groups=mesh['section'=8,'chan'=32] {'chan'}, use_global_device_ids=true, to_apply=%region_2.2 | all-reduce | flops 64 | bytes 512 | tf_op jit(solution)/shard_map/while/body/eval_jaxpr/psum | solution.py:69
  199.4 17.3 %all-to-all-done = bf16[32,64,256]{2,1,0:T(8,128)(2,1)S(1)} async-done(((bf16[32,64,256]{2,1,0:T(8,128)(2,1)}), bf16[32,64,256]{2,1,0:T(8,128)(2,1)S(1)}, u32[]{:S(2)}, u32[]{:S(2)}) %all-to-all-start) | async-done | bytes 1048608 | tf_op jit(solution)/shard_map/while/body/eval_jaxpr/all_to_all | solution.py:13
  225.6 19.4 %collective-permute-start = (bf16[64,256]{1,0:T(8,128)(2,1)S(1)}, bf16[64,256]{1,0:T(8,128)(2,1)S(1)}, u32[]{:S(2)}, u32[]{:S(2)}) collective-permute-start(bf16[64,256]{1,0:T(8,128)(2,1)S(1)} %get-tuple-element.581), channel_id=1, source_target_pairs={{0,32},{32,64},{64,96},{96,128},{128,160},{160,192},{192,224},{1,3... | collective-permute-start | bytes 98312 | tf_op jit(solution)/shard_map/while/body/eval_jaxpr/ppermute | solution.py:19
  248.0 57.2 %psum.12 = f32[64]{0:T(128)S(1)} all-reduce(f32[64]{0:T(128)S(1)} %get-tuple-element.574), channel_id=1, replica_groups=mesh['section'=8,'chan'=32] {'chan'}, use_global_device_ids=true, to_apply=%region_2.2 | all-reduce | flops 64 | bytes 512 | tf_op jit(solution)/shard_map/while/body/eval_jaxpr/psum | solution.py:69
  311.8 17.1 %all-to-all-done = bf16[32,64,256]{2,1,0:T(8,128)(2,1)S(1)} async-done(((bf16[32,64,256]{2,1,0:T(8,128)(2,1)}), bf16[32,64,256]{2,1,0:T(8,128)(2,1)S(1)}, u32[]{:S(2)}, u32[]{:S(2)}) %all-to-all-start) | async-done | bytes 1048608 | tf_op jit(solution)/shard_map/while/body/eval_jaxpr/all_to_all | solution.py:13
  337.8 20.1 %collective-permute-start = (bf16[64,256]{1,0:T(8,128)(2,1)S(1)}, bf16[64,256]{1,0:T(8,128)(2,1)S(1)}, u32[]{:S(2)}, u32[]{:S(2)}) collective-permute-start(bf16[64,256]{1,0:T(8,128)(2,1)S(1)} %get-tuple-element.581), channel_id=1, source_target_pairs={{0,32},{32,64},{64,96},{96,128},{128,160},{160,192},{192,224},{1,3... | collective-permute-start | bytes 98312 | tf_op jit(solution)/shard_map/while/body/eval_jaxpr/ppermute | solution.py:19
  360.9 57.2 %psum.12 = f32[64]{0:T(128)S(1)} all-reduce(f32[64]{0:T(128)S(1)} %get-tuple-element.574), channel_id=1, replica_groups=mesh['section'=8,'chan'=32] {'chan'}, use_global_device_ids=true, to_apply=%region_2.2 | all-reduce | flops 64 | bytes 512 | tf_op jit(solution)/shard_map/while/body/eval_jaxpr/psum | solution.py:69
  425.2 18.5 %all-to-all-done = bf16[32,64,256]{2,1,0:T(8,128)(2,1)S(1)} async-done(((bf16[32,64,256]{2,1,0:T(8,128)(2,1)}), bf16[32,64,256]{2,1,0:T(8,128)(2,1)S(1)}, u32[]{:S(2)}, u32[]{:S(2)}) %all-to-all-start) | async-done | bytes 1048608 | tf_op jit(solution)/shard_map/while/body/eval_jaxpr/all_to_all | solution.py:13
  452.6 18.1 %collective-permute-start = (bf16[64,256]{1,0:T(8,128)(2,1)S(1)}, bf16[64,256]{1,0:T(8,128)(2,1)S(1)}, u32[]{:S(2)}, u32[]{:S(2)}) collective-permute-start(bf16[64,256]{1,0:T(8,128)(2,1)S(1)} %get-tuple-element.581), channel_id=1, source_target_pairs={{0,32},{32,64},{64,96},{96,128},{128,160},{160,192},{192,224},{1,3... | collective-permute-start | bytes 98312 | tf_op jit(solution)/shard_map/while/body/eval_jaxpr/ppermute | solution.py:19
  473.7 57.1 %psum.12 = f32[64]{0:T(128)S(1)} all-reduce(f32[64]{0:T(128)S(1)} %get-tuple-element.574), channel_id=1, replica_groups=mesh['section'=8,'chan'=32] {'chan'}, use_global_device_ids=true, to_apply=%region_2.2 | all-reduce | flops 64 | bytes 512 | tf_op jit(solution)/shard_map/while/body/eval_jaxpr/psum | solution.py:69
  538.0 19.7 %all-to-all-done = bf16[32,64,256]{2,1,0:T(8,128)(2,1)S(1)} async-done(((bf16[32,64,256]{2,1,0:T(8,128)(2,1)}), bf16[32,64,256]{2,1,0:T(8,128)(2,1)S(1)}, u32[]{:S(2)}, u32[]{:S(2)}) %all-to-all-start) | async-done | bytes 1048608 | tf_op jit(solution)/shard_map/while/body/eval_jaxpr/all_to_all | solution.py:13
  566.5 17.6 %collective-permute-start = (bf16[64,256]{1,0:T(8,128)(2,1)S(1)}, bf16[64,256]{1,0:T(8,128)(2,1)S(1)}, u32[]{:S(2)}, u32[]{:S(2)}) collective-permute-start(bf16[64,256]{1,0:T(8,128)(2,1)S(1)} %get-tuple-element.581), channel_id=1, source_target_pairs={{0,32},{32,64},{64,96},{96,128},{128,160},{160,192},{192,224},{1,3... | collective-permute-start | bytes 98312 | tf_op jit(solution)/shard_map/while/body/eval_jaxpr/ppermute | solution.py:19
  587.1 57.1 %psum.12 = f32[64]{0:T(128)S(1)} all-reduce(f32[64]{0:T(128)S(1)} %get-tuple-element.574), channel_id=1, replica_groups=mesh['section'=8,'chan'=32] {'chan'}, use_global_device_ids=true, to_apply=%region_2.2 | all-reduce | flops 64 | bytes 512 | tf_op jit(solution)/shard_map/while/body/eval_jaxpr/psum | solution.py:69
  651.5 20.9 %all-to-all-done = bf16[32,64,256]{2,1,0:T(8,128)(2,1)S(1)} async-done(((bf16[32,64,256]{2,1,0:T(8,128)(2,1)}), bf16[32,64,256]{2,1,0:T(8,128)(2,1)S(1)}, u32[]{:S(2)}, u32[]{:S(2)}) %all-to-all-start) | async-done | bytes 1048608 | tf_op jit(solution)/shard_map/while/body/eval_jaxpr/all_to_all | solution.py:13
  700.5 57.1 %psum.12 = f32[64]{0:T(128)S(1)} all-reduce(f32[64]{0:T(128)S(1)} %get-tuple-element.574), channel_id=1, replica_groups=mesh['section'=8,'chan'=32] {'chan'}, use_global_device_ids=true, to_apply=%region_2.2 | all-reduce | flops 64 | bytes 512 | tf_op jit(solution)/shard_map/while/body/eval_jaxpr/psum | solution.py:69
  764.3 20.0 %all-to-all-done = bf16[32,64,256]{2,1,0:T(8,128)(2,1)S(1)} async-done(((bf16[32,64,256]{2,1,0:T(8,128)(2,1)}), bf16[32,64,256]{2,1,0:T(8,128)(2,1)S(1)}, u32[]{:S(2)}, u32[]{:S(2)}) %all-to-all-start) | async-done | bytes 1048608 | tf_op jit(solution)/shard_map/while/body/eval_jaxpr/all_to_all | solution.py:13
  793.1 17.1 %collective-permute-start = (bf16[64,256]{1,0:T(8,128)(2,1)S(1)}, bf16[64,256]{1,0:T(8,128)(2,1)S(1)}, u32[]{:S(2)}, u32[]{:S(2)}) collective-permute-start(bf16[64,256]{1,0:T(8,128)(2,1)S(1)} %get-tuple-element.581), channel_id=1, source_target_pairs={{0,32},{32,64},{64,96},{96,128},{128,160},{160,192},{192,224},{1,3... | collective-permute-start | bytes 98312 | tf_op jit(solution)/shard_map/while/body/eval_jaxpr/ppermute | solution.py:19
  813.3 57.2 %psum.12 = f32[64]{0:T(128)S(1)} all-reduce(f32[64]{0:T(128)S(1)} %get-tuple-element.574), channel_id=1, replica_groups=mesh['section'=8,'chan'=32] {'chan'}, use_global_device_ids=true, to_apply=%region_2.2 | all-reduce | flops 64 | bytes 512 | tf_op jit(solution)/shard_map/while/body/eval_jaxpr/psum | solution.py:69
  877.1 20.3 %all-to-all-done = bf16[32,64,256]{2,1,0:T(8,128)(2,1)S(1)} async-done(((bf16[32,64,256]{2,1,0:T(8,128)(2,1)}), bf16[32,64,256]{2,1,0:T(8,128)(2,1)S(1)}, u32[]{:S(2)}, u32[]{:S(2)}) %all-to-all-start) | async-done | bytes 1048608 | tf_op jit(solution)/shard_map/while/body/eval_jaxpr/all_to_all | solution.py:13
  906.3 16.8 %collective-permute-start = (bf16[64,256]{1,0:T(8,128)(2,1)S(1)}, bf16[64,256]{1,0:T(8,128)(2,1)S(1)}, u32[]{:S(2)}, u32[]{:S(2)}) collective-permute-start(bf16[64,256]{1,0:T(8,128)(2,1)S(1)} %get-tuple-element.581), channel_id=1, source_target_pairs={{0,32},{32,64},{64,96},{96,128},{128,160},{160,192},{192,224},{1,3... | collective-permute-start | bytes 98312 | tf_op jit(solution)/shard_map/while/body/eval_jaxpr/ppermute | solution.py:19
  926.1 57.2 %psum.12 = f32[64]{0:T(128)S(1)} all-reduce(f32[64]{0:T(128)S(1)} %get-tuple-element.574), channel_id=1, replica_groups=mesh['section'=8,'chan'=32] {'chan'}, use_global_device_ids=true, to_apply=%region_2.2 | all-reduce | flops 64 | bytes 512 | tf_op jit(solution)/shard_map/while/body/eval_jaxpr/psum | solution.py:69
  989.9 20.3 %all-to-all-done = bf16[32,64,256]{2,1,0:T(8,128)(2,1)S(1)} async-done(((bf16[32,64,256]{2,1,0:T(8,128)(2,1)}), bf16[32,64,256]{2,1,0:T(8,128)(2,1)S(1)}, u32[]{:S(2)}, u32[]{:S(2)}) %all-to-all-start) | async-done | bytes 1048608 | tf_op jit(solution)/shard_map/while/body/eval_jaxpr/all_to_all | solution.py:13
  1019.1 17.4 %collective-permute-start = (bf16[64,256]{1,0:T(8,128)(2,1)S(1)}, bf16[64,256]{1,0:T(8,128)(2,1)S(1)}, u32[]{:S(2)}, u32[]{:S(2)}) collective-permute-start(bf16[64,256]{1,0:T(8,128)(2,1)S(1)} %get-tuple-element.581), channel_id=1, source_target_pairs={{0,32},{32,64},{64,96},{96,128},{128,160},{160,192},{192,224},{1,3... | collective-permute-start | bytes 98312 | tf_op jit(solution)/shard_map/while/body/eval_jaxpr/ppermute | solution.py:19
  1039.5 57.5 %psum.12 = f32[64]{0:T(128)S(1)} all-reduce(f32[64]{0:T(128)S(1)} %get-tuple-element.574), channel_id=1, replica_groups=mesh['section'=8,'chan'=32] {'chan'}, use_global_device_ids=true, to_apply=%region_2.2 | all-reduce | flops 64 | bytes 512 | tf_op jit(solution)/shard_map/while/body/eval_jaxpr/psum | solution.py:69
  1103.4 20.9 %all-to-all-done = bf16[32,64,256]{2,1,0:T(8,128)(2,1)S(1)} async-done(((bf16[32,64,256]{2,1,0:T(8,128)(2,1)}), bf16[32,64,256]{2,1,0:T(8,128)(2,1)S(1)}, u32[]{:S(2)}, u32[]{:S(2)}) %all-to-all-start) | async-done | bytes 1048608 | tf_op jit(solution)/shard_map/while/body/eval_jaxpr/all_to_all | solution.py:13
  1152.4 57.2 %psum.12 = f32[64]{0:T(128)S(1)} all-reduce(f32[64]{0:T(128)S(1)} %get-tuple-element.574), channel_id=1, replica_groups=mesh['section'=8,'chan'=32] {'chan'}, use_global_device_ids=true, to_apply=%region_2.2 | all-reduce | flops 64 | bytes 512 | tf_op jit(solution)/shard_map/while/body/eval_jaxpr/psum | solution.py:69
  1216.2 19.8 %all-to-all-done = bf16[32,64,256]{2,1,0:T(8,128)(2,1)S(1)} async-done(((bf16[32,64,256]{2,1,0:T(8,128)(2,1)}), bf16[32,64,256]{2,1,0:T(8,128)(2,1)S(1)}, u32[]{:S(2)}, u32[]{:S(2)}) %all-to-all-start) | async-done | bytes 1048608 | tf_op jit(solution)/shard_map/while/body/eval_jaxpr/all_to_all | solution.py:13
  1244.8 17.8 %collective-permute-start = (bf16[64,256]{1,0:T(8,128)(2,1)S(1)}, bf16[64,256]{1,0:T(8,128)(2,1)S(1)}, u32[]{:S(2)}, u32[]{:S(2)}) collective-permute-start(bf16[64,256]{1,0:T(8,128)(2,1)S(1)} %get-tuple-element.581), channel_id=1, source_target_pairs={{0,32},{32,64},{64,96},{96,128},{128,160},{160,192},{192,224},{1,3... | collective-permute-start | bytes 98312 | tf_op jit(solution)/shard_map/while/body/eval_jaxpr/ppermute | solution.py:19
  (301 shorter events, 239.1 us)
Async XLA Ops:
  17.4 16.7 %copy-start.4 = (f32[1,16,16]{2,1,0:T(8,128)S(1)}, f32[1,16,16]{2,1,0:T(8,128)}, u32[]{:S(2)}) copy-start(f32[1,16,16]{2,1,0:T(8,128)} %param.15) | copy-start | bytes 3076
  17.4 16.8 %copy-start.1 = (f32[1,16,16]{2,1,0:T(8,128)S(1)}, f32[1,16,16]{2,1,0:T(8,128)}, u32[]{:S(2)}) copy-start(f32[1,16,16]{2,1,0:T(8,128)} %param.14) | copy-start | bytes 3076
  34.1 46.8 %copy-start.3 = (f32[1,128,16]{1,2,0:T(8,128)S(1)}, f32[1,128,16]{1,2,0:T(8,128)}, u32[]{:S(2)}) copy-start(f32[1,128,16]{1,2,0:T(8,128)} %param.13) | copy-start | bytes 24580
  76.0 51.8 %copy-start.2 = (bf16[1,256]{1,0:T(2,128)(2,1)S(1)}, bf16[1,256]{1,0:T(2,128)(2,1)}, u32[]{:S(2)}) copy-start(bf16[1,256]{1,0:T(2,128)(2,1)} %param.10) | copy-start | bytes 1540
  195.4 21.3 %all-to-all-start = ((bf16[32,64,256]{2,1,0:T(8,128)(2,1)}), bf16[32,64,256]{2,1,0:T(8,128)(2,1)S(1)}, u32[]{:S(2)}, u32[]{:S(2)}) async-start(bf16[32,64,256]{2,1,0:T(8,128)(2,1)} %stack.6), calls=%async_computation | async-start | bytes 2097152 | tf_op jit(solution)/shard_map/while/body/eval_jaxpr/all_to_all | solution.py:13
  225.6 20.4 %collective-permute-start = (bf16[64,256]{1,0:T(8,128)(2,1)S(1)}, bf16[64,256]{1,0:T(8,128)(2,1)S(1)}, u32[]{:S(2)}, u32[]{:S(2)}) collective-permute-start(bf16[64,256]{1,0:T(8,128)(2,1)S(1)} %get-tuple-element.581), channel_id=1, source_target_pairs={{0,32},{32,64},{64,96},{96,128},{128,160},{160,192},{192,224},{1,3... | collective-permute-start | bytes 98312 | tf_op jit(solution)/shard_map/while/body/eval_jaxpr/ppermute | solution.py:19
  306.4 22.5 %all-to-all-start = ((bf16[32,64,256]{2,1,0:T(8,128)(2,1)}), bf16[32,64,256]{2,1,0:T(8,128)(2,1)S(1)}, u32[]{:S(2)}, u32[]{:S(2)}) async-start(bf16[32,64,256]{2,1,0:T(8,128)(2,1)} %stack.6), calls=%async_computation | async-start | bytes 2097152 | tf_op jit(solution)/shard_map/while/body/eval_jaxpr/all_to_all | solution.py:13
  337.8 21.1 %collective-permute-start = (bf16[64,256]{1,0:T(8,128)(2,1)S(1)}, bf16[64,256]{1,0:T(8,128)(2,1)S(1)}, u32[]{:S(2)}, u32[]{:S(2)}) collective-permute-start(bf16[64,256]{1,0:T(8,128)(2,1)S(1)} %get-tuple-element.581), channel_id=1, source_target_pairs={{0,32},{32,64},{64,96},{96,128},{128,160},{160,192},{192,224},{1,3... | collective-permute-start | bytes 98312 | tf_op jit(solution)/shard_map/while/body/eval_jaxpr/ppermute | solution.py:19
  419.4 24.3 %all-to-all-start = ((bf16[32,64,256]{2,1,0:T(8,128)(2,1)}), bf16[32,64,256]{2,1,0:T(8,128)(2,1)S(1)}, u32[]{:S(2)}, u32[]{:S(2)}) async-start(bf16[32,64,256]{2,1,0:T(8,128)(2,1)} %stack.6), calls=%async_computation | async-start | bytes 2097152 | tf_op jit(solution)/shard_map/while/body/eval_jaxpr/all_to_all | solution.py:13
  452.6 19.1 %collective-permute-start = (bf16[64,256]{1,0:T(8,128)(2,1)S(1)}, bf16[64,256]{1,0:T(8,128)(2,1)S(1)}, u32[]{:S(2)}, u32[]{:S(2)}) collective-permute-start(bf16[64,256]{1,0:T(8,128)(2,1)S(1)} %get-tuple-element.581), channel_id=1, source_target_pairs={{0,32},{32,64},{64,96},{96,128},{128,160},{160,192},{192,224},{1,3... | collective-permute-start | bytes 98312 | tf_op jit(solution)/shard_map/while/body/eval_jaxpr/ppermute | solution.py:19
  532.1 25.5 %all-to-all-start = ((bf16[32,64,256]{2,1,0:T(8,128)(2,1)}), bf16[32,64,256]{2,1,0:T(8,128)(2,1)S(1)}, u32[]{:S(2)}, u32[]{:S(2)}) async-start(bf16[32,64,256]{2,1,0:T(8,128)(2,1)} %stack.6), calls=%async_computation | async-start | bytes 2097152 | tf_op jit(solution)/shard_map/while/body/eval_jaxpr/all_to_all | solution.py:13
  566.5 18.6 %collective-permute-start = (bf16[64,256]{1,0:T(8,128)(2,1)S(1)}, bf16[64,256]{1,0:T(8,128)(2,1)S(1)}, u32[]{:S(2)}, u32[]{:S(2)}) collective-permute-start(bf16[64,256]{1,0:T(8,128)(2,1)S(1)} %get-tuple-element.581), channel_id=1, source_target_pairs={{0,32},{32,64},{64,96},{96,128},{128,160},{160,192},{192,224},{1,3... | collective-permute-start | bytes 98312 | tf_op jit(solution)/shard_map/while/body/eval_jaxpr/ppermute | solution.py:19
  645.5 26.9 %all-to-all-start = ((bf16[32,64,256]{2,1,0:T(8,128)(2,1)}), bf16[32,64,256]{2,1,0:T(8,128)(2,1)S(1)}, u32[]{:S(2)}, u32[]{:S(2)}) async-start(bf16[32,64,256]{2,1,0:T(8,128)(2,1)} %stack.6), calls=%async_computation | async-start | bytes 2097152 | tf_op jit(solution)/shard_map/while/body/eval_jaxpr/all_to_all | solution.py:13
  681.3 17.2 %collective-permute-start = (bf16[64,256]{1,0:T(8,128)(2,1)S(1)}, bf16[64,256]{1,0:T(8,128)(2,1)S(1)}, u32[]{:S(2)}, u32[]{:S(2)}) collective-permute-start(bf16[64,256]{1,0:T(8,128)(2,1)S(1)} %get-tuple-element.581), channel_id=1, source_target_pairs={{0,32},{32,64},{64,96},{96,128},{128,160},{160,192},{192,224},{1,3... | collective-permute-start | bytes 98312 | tf_op jit(solution)/shard_map/while/body/eval_jaxpr/ppermute | solution.py:19
  758.9 25.4 %all-to-all-start = ((bf16[32,64,256]{2,1,0:T(8,128)(2,1)}), bf16[32,64,256]{2,1,0:T(8,128)(2,1)S(1)}, u32[]{:S(2)}, u32[]{:S(2)}) async-start(bf16[32,64,256]{2,1,0:T(8,128)(2,1)} %stack.6), calls=%async_computation | async-start | bytes 2097152 | tf_op jit(solution)/shard_map/while/body/eval_jaxpr/all_to_all | solution.py:13
  793.1 18.1 %collective-permute-start = (bf16[64,256]{1,0:T(8,128)(2,1)S(1)}, bf16[64,256]{1,0:T(8,128)(2,1)S(1)}, u32[]{:S(2)}, u32[]{:S(2)}) collective-permute-start(bf16[64,256]{1,0:T(8,128)(2,1)S(1)} %get-tuple-element.581), channel_id=1, source_target_pairs={{0,32},{32,64},{64,96},{96,128},{128,160},{160,192},{192,224},{1,3... | collective-permute-start | bytes 98312 | tf_op jit(solution)/shard_map/while/body/eval_jaxpr/ppermute | solution.py:19
  871.8 25.6 %all-to-all-start = ((bf16[32,64,256]{2,1,0:T(8,128)(2,1)}), bf16[32,64,256]{2,1,0:T(8,128)(2,1)S(1)}, u32[]{:S(2)}, u32[]{:S(2)}) async-start(bf16[32,64,256]{2,1,0:T(8,128)(2,1)} %stack.6), calls=%async_computation | async-start | bytes 2097152 | tf_op jit(solution)/shard_map/while/body/eval_jaxpr/all_to_all | solution.py:13
  906.3 17.8 %collective-permute-start = (bf16[64,256]{1,0:T(8,128)(2,1)S(1)}, bf16[64,256]{1,0:T(8,128)(2,1)S(1)}, u32[]{:S(2)}, u32[]{:S(2)}) collective-permute-start(bf16[64,256]{1,0:T(8,128)(2,1)S(1)} %get-tuple-element.581), channel_id=1, source_target_pairs={{0,32},{32,64},{64,96},{96,128},{128,160},{160,192},{192,224},{1,3... | collective-permute-start | bytes 98312 | tf_op jit(solution)/shard_map/while/body/eval_jaxpr/ppermute | solution.py:19
  984.6 25.7 %all-to-all-start = ((bf16[32,64,256]{2,1,0:T(8,128)(2,1)}), bf16[32,64,256]{2,1,0:T(8,128)(2,1)S(1)}, u32[]{:S(2)}, u32[]{:S(2)}) async-start(bf16[32,64,256]{2,1,0:T(8,128)(2,1)} %stack.6), calls=%async_computation | async-start | bytes 2097152 | tf_op jit(solution)/shard_map/while/body/eval_jaxpr/all_to_all | solution.py:13
  1019.1 18.4 %collective-permute-start = (bf16[64,256]{1,0:T(8,128)(2,1)S(1)}, bf16[64,256]{1,0:T(8,128)(2,1)S(1)}, u32[]{:S(2)}, u32[]{:S(2)}) collective-permute-start(bf16[64,256]{1,0:T(8,128)(2,1)S(1)} %get-tuple-element.581), channel_id=1, source_target_pairs={{0,32},{32,64},{64,96},{96,128},{128,160},{160,192},{192,224},{1,3... | collective-permute-start | bytes 98312 | tf_op jit(solution)/shard_map/while/body/eval_jaxpr/ppermute | solution.py:19
  1098.3 26.0 %all-to-all-start = ((bf16[32,64,256]{2,1,0:T(8,128)(2,1)}), bf16[32,64,256]{2,1,0:T(8,128)(2,1)S(1)}, u32[]{:S(2)}, u32[]{:S(2)}) async-start(bf16[32,64,256]{2,1,0:T(8,128)(2,1)} %stack.6), calls=%async_computation | async-start | bytes 2097152 | tf_op jit(solution)/shard_map/while/body/eval_jaxpr/all_to_all | solution.py:13
  1133.1 17.2 %collective-permute-start = (bf16[64,256]{1,0:T(8,128)(2,1)S(1)}, bf16[64,256]{1,0:T(8,128)(2,1)S(1)}, u32[]{:S(2)}, u32[]{:S(2)}) collective-permute-start(bf16[64,256]{1,0:T(8,128)(2,1)S(1)} %get-tuple-element.581), channel_id=1, source_target_pairs={{0,32},{32,64},{64,96},{96,128},{128,160},{160,192},{192,224},{1,3... | collective-permute-start | bytes 98312 | tf_op jit(solution)/shard_map/while/body/eval_jaxpr/ppermute | solution.py:19
  1210.8 25.1 %all-to-all-start = ((bf16[32,64,256]{2,1,0:T(8,128)(2,1)}), bf16[32,64,256]{2,1,0:T(8,128)(2,1)S(1)}, u32[]{:S(2)}, u32[]{:S(2)}) async-start(bf16[32,64,256]{2,1,0:T(8,128)(2,1)} %stack.6), calls=%async_computation | async-start | bytes 2097152 | tf_op jit(solution)/shard_map/while/body/eval_jaxpr/all_to_all | solution.py:13
  1244.8 18.8 %collective-permute-start = (bf16[64,256]{1,0:T(8,128)(2,1)S(1)}, bf16[64,256]{1,0:T(8,128)(2,1)S(1)}, u32[]{:S(2)}, u32[]{:S(2)}) collective-permute-start(bf16[64,256]{1,0:T(8,128)(2,1)S(1)} %get-tuple-element.581), channel_id=1, source_target_pairs={{0,32},{32,64},{64,96},{96,128},{128,160},{160,192},{192,224},{1,3... | collective-permute-start | bytes 98312 | tf_op jit(solution)/shard_map/while/body/eval_jaxpr/ppermute | solution.py:19
  1263.6 0.6 copy-start
